TPU v7x, 256 devices: a whole 4x4x8 slice. The times are simulated.
256 devices in a mesh: pipe: 4 (over y_hi, core), ctx: 8 (over y_lo, x), tp: 8 (over z).
Axes of the slice: x: 4, y: 4 (y_hi: 2, y_lo: 2; y = y_hi * 2 + y_lo), z: 8, core: 2. Of those that a mesh axis runs over, the one named last changes fastest.
Arguments:
- section_input: bfloat16 [4, 1024, 8192], P('pipe', 'tp', 'ctx'), may hold values from -42 to 42, as said below
- norm_gain: bfloat16 [4, 8192], P('pipe', 'ctx'), may hold values from 0.099609375 to 1.8984375
- in_weight: bfloat16 [4, 8192, 3, 8192], P('pipe', 'ctx', None, 'tp'), may hold values from -0.0625 to 0.0625
- qkv_filters: bfloat16 [4, 3, 128, 8192], P('pipe', None, None, 'tp'), may hold values from -0.5 to 0.5
- mix_filter: bfloat16 [4, 128, 8192], P('pipe', None, 'tp'), may hold values from -0.5 to 0.5
- out_weight: bfloat16 [4, 8192, 8192], P('pipe', 'tp', 'ctx'), may hold values from -0.0625 to 0.0625
Outputs:
- handed: bfloat16 [4, 1024, 8192], P('pipe', 'tp', 'ctx')
Inputs may be any that keep to these rules, and one draw needn't show every extreme that they name: `section_input`: Real-valued activations with position and feature scales of order one.
All inputs are finite; a program needn't handle non-finite values.
Results may differ from a plain program's by a relative error of at most 0.029.
Values may be sent and summed in bfloat16 or wider, within the bound.
No kernel may reach another device: no remote copies, remote signals or barrier semaphores. Data moves between devices by JAX's collectives and lax.ppermute only.
A program may use at most 128 MiB of HBM per device.

v0:
```python
import jax
import jax.numpy as jnp
from jax import lax
from jax.sharding import PartitionSpec as P

D = 8192
NORM_EPS = 1e-05


def passed_along(value, axis, steps):
    count = lax.axis_size(axis)
    first, last = (max(0, -steps), min(count, count - steps))
    return lax.ppermute(value, axis, [(source, source + steps) for source in range(first, last)])


def shifted(value, axis, steps):
    count = lax.axis_size(axis)
    pairs = [(source, (source + steps) % count) for source in range(count)]
    return lax.ppermute(value, axis, pairs)


def causal_mix(padded, tap_weights):
    channels = tap_weights.shape[1]
    kernel = tap_weights[::-1][:, None, :]
    result = lax.conv_general_dilated(
        padded[None],
        kernel,
        (1,),
        "VALID",
        dimension_numbers=("NWC", "WIO", "NWC"),
        feature_group_count=channels,
        precision=lax.Precision.HIGHEST,
    )
    return result[0]


def on_device(section_input, norm_gain, in_weight, qkv_filters, mix_filter, out_weight):
    incoming = section_input[0].astype(jnp.float32)
    squares = lax.psum(jnp.sum(incoming * incoming, axis=1), "ctx")
    normed = (
        incoming * lax.rsqrt(squares[:, None] / D + NORM_EPS) * norm_gain[0].astype(jnp.float32)
    ).astype(jnp.bfloat16)
    gathered = lax.all_gather(normed, "tp", axis=0, tiled=True)
    width_in = in_weight.shape[1]
    channels = in_weight.shape[3]
    weight_in = in_weight[0].reshape(width_in, 3 * channels)
    weight_out = out_weight[0]
    tap_count = qkv_filters.shape[2]
    filters_qkv = qkv_filters[0].astype(jnp.float32)
    filters_mix = mix_filter[0].astype(jnp.float32)
    total_rows = gathered.shape[0]
    seg_rows = total_rows // lax.axis_size("ctx")
    projected = lax.psum_scatter(
        jnp.dot(gathered, weight_in, preferred_element_type=jnp.float32).astype(jnp.bfloat16),
        "ctx",
        scatter_dimension=0,
        tiled=True,
    )
    prior_rows = passed_along(projected[seg_rows - (tap_count - 1) :], "ctx", 1)
    padded = jnp.concatenate([prior_rows, projected], 0).astype(jnp.float32)
    table_qkv = jnp.transpose(filters_qkv, (1, 0, 2)).reshape(tap_count, 3 * channels)
    filtered = causal_mix(padded, table_qkv).reshape(seg_rows, 3, channels)
    product = (filtered[:, 1] * filtered[:, 2]).astype(jnp.bfloat16)
    prior_prod = passed_along(product[seg_rows - (tap_count - 1) :], "ctx", 1)
    mixed_sig = causal_mix(
        jnp.concatenate([prior_prod, product], 0).astype(jnp.float32), filters_mix
    )
    gated_out = (filtered[:, 0] * mixed_sig).astype(jnp.bfloat16)
    partial_value = jnp.dot(
        lax.all_gather(gated_out, "ctx", axis=0, tiled=True),
        weight_out,
        preferred_element_type=jnp.float32,
    )
    summed = lax.psum_scatter(
        partial_value.astype(jnp.bfloat16), "tp", scatter_dimension=0, tiled=True
    ).astype(jnp.float32)
    block_out = (incoming + summed).astype(jnp.bfloat16)
    handed = shifted(block_out, "pipe", 1)
    return handed[None]


def solution(mesh):
    return jax.shard_map(
        on_device,
        mesh=mesh,
        in_specs=(
            P("pipe", "tp", "ctx"),
            P("pipe", "ctx"),
            P("pipe", "ctx", None, "tp"),
            P("pipe", None, None, "tp"),
            P("pipe", None, "tp"),
            P("pipe", "tp", "ctx"),
        ),
        out_specs=P("pipe", "tp", "ctx"),
        check_vma=False,
    )
```

profile of v0, /device:TPU:1, one launch (start us, length us, event | category | flops | bytes accessed | tf_op | source)
XLA Modules:
  0.0 338.4 jit_solution(3435110821669046357)
XLA Ops:
  6.5 0.8 mul.40
  7.4 1.1 fusion.7
  8.5 16.8 %psum.7 = f32[128]{0:T(128)S(1)} all-reduce(f32[128]{0:T(128)S(1)} %fusion.7), channel_id=1, replica_groups=mesh['pipe'=4,'ctx'=8,'tp'=8] {'ctx'}, use_global_device_ids=true, to_apply=%region_1.0 | all-reduce | flops 128 | bytes 1024 | tf_op jit(solution)/shard_map/psum | solution.py:39
  25.2 1.8 fusion.9
  27.1 8.7 %copy.12 = bf16[1,1024,3,1024]{1,3,2,0:T(8,128)(2,1)} copy(bf16[1,1024,3,1024]{3,1,2,0:T(8,128)(2,1)} %param.8) | data formatting | bytes 12582912 | tf_op args[2]
  35.8 32.1 %all-gather.3.cloned.1.call-done = bf16[1024,1024]{1,0:T(8,128)(2,1)} async-done(((bf16[128,1024]{1,0:T(8,128)(2,1)}), bf16[1024,1024]{1,0:T(8,128)(2,1)}) %all-gather.3.cloned.1.call-update) | async-done | bytes 2097168 | tf_op jit(solution)/shard_map/all_gather | solution.py:43
  67.9 11.3 %convolution_convert_fusion = bf16[1024,3072]{1,0:T(8,128)(2,1)} fusion(bf16[1024,1024]{1,0:T(8,128)(2,1)} %all-gather.3.cloned.1.call-done, bf16[1024,3072]{0,1:T(8,128)(2,1)} %bitcast.43), kind=kOutput, calls=%fused_computation | convolution fusion | flops 6445596672 | bytes 14680064 | tf_op jit(solution)/shard_map/dot_general | solution.py:54
  79.2 78.2 %reduce-scatter.3.cloned.1.call-done = bf16[128,3072]{1,0:T(8,128)(2,1)} async-done(((bf16[1024,3072]{1,0:T(8,128)(2,1)}), bf16[128,3072]{1,0:T(8,128)(2,1)}) %reduce-scatter.3.cloned.1.call-update) | async-done | bytes 786448 | tf_op jit(solution)/shard_map/reduce_scatter | solution.py:53
  157.5 2.2 slice.24
  159.7 2.2 collective-permute-start
  161.8 1.5 copy.13
  163.4 1.3 bitcast_convert_fusion
  164.6 13.3 %rev.6 = f32[128,3072]{0,1:T(8,128)} reverse(f32[128,3072]{0,1:T(8,128)} %bitcast.45), dimensions={0} | reverse | bytes 3145728 | tf_op jit(solution)/shard_map/rev | solution.py:24
  177.9 4.6 %copy.15 = f32[128,1,3072]{2,1,0:T(1,128)} copy(f32[128,1,3072]{0,2,1:T(8,128)} %bitcast.46) | data formatting | bytes 3145728 | tf_op jit(solution)/shard_map/broadcast_in_dim | solution.py:24
  182.5 1.5 maximum_bitcast_fusion
  184.2 17.5 %fusion = f32[1,128,3072]{2,0,1:T(1,128)} fusion(f32[128,1,3072]{2,1,0:T(1,128)S(1)} %copy-done.3, bf16[1,255,3072]{2,1,0:T(8,128)(2,1)S(1)} %maximum_bitcast_fusion), kind=kOutput, calls=%fused_computation.1 | convolution fusion | flops 603979776 | bytes 4712448 | tf_op jit(solution)/shard_map/conv_general_dilated | solution.py:25
  201.7 4.4 %copy.16 = f32[1,128,3072]{1,2,0:T(8,128)} copy(f32[1,128,3072]{2,0,1:T(1,128)} %fusion) | data formatting | bytes 3145728 | tf_op jit(solution)/shard_map/conv_general_dilated | solution.py:25
  206.1 2.3 fusion.15
  208.4 0.8 slice_bitcast_fusion
  209.2 2.3 collective-permute-start.1
  211.5 2.7 rev.7
  214.2 1.2 copy.24
  215.7 1.2 maximum_bitcast_fusion.1
  216.9 2.1 copy.19
  219.0 7.3 %fusion.13 = f32[1,128,1024]{2,0,1:T(1,128)S(1)} fusion(bf16[1,255,1024]{2,0,1:T(2,128)(2,1)} %copy.19, f32[128,1,1024]{2,0,1:T(8,128)} %bitcast.48), kind=kOutput, calls=%fused_computation.20 | convolution fusion | flops 201326592 | bytes 1570816 | tf_op jit(solution)/shard_map/conv_general_dilated | solution.py:25
  226.3 0.8 fusion.12
  227.2 43.2 %all-gather.5.cloned.1.call-done = bf16[1024,1024]{1,0:T(8,128)(2,1)} async-done(((bf16[128,1024]{1,0:T(8,128)(2,1)}), bf16[1024,1024]{1,0:T(8,128)(2,1)}) %all-gather.5.cloned.1.call-update) | async-done | bytes 2097168 | tf_op jit(solution)/shard_map/all_gather | solution.py:70
  270.4 5.3 %fusion.4 = bf16[1024,1024]{1,0:T(8,128)(2,1)} fusion(bf16[1024,1024]{1,0:T(8,128)(2,1)} %all-gather.5.cloned.1.call-done, bf16[1,1024,1024]{2,1,0:T(8,128)(2,1)S(1)} %copy-done), kind=kOutput, calls=%fused_computation.5 | convolution fusion | flops 2148532224 | bytes 6291456 | tf_op jit(solution)/shard_map/dot_general | solution.py:69
  275.7 43.1 %reduce-scatter.5.cloned.1.call-done = bf16[128,1024]{1,0:T(8,128)(2,1)} async-done(((bf16[1024,1024]{1,0:T(8,128)(2,1)}), bf16[128,1024]{1,0:T(8,128)(2,1)}) %reduce-scatter.5.cloned.1.call-update) | async-done | bytes 262160 | tf_op jit(solution)/shard_map/reduce_scatter | solution.py:74
  318.8 1.0 fusion.10
  319.8 8.0 %collective-permute-start.2 = (bf16[128,1024]{1,0:T(8,128)(2,1)S(1)}, bf16[128,1024]{1,0:T(8,128)(2,1)S(1)}, u32[]{:S(2)}, u32[]{:S(2)}) collective-permute-start(bf16[128,1024]{1,0:T(8,128)(2,1)S(1)} %fusion.10), channel_id=1, source_target_pairs={{0,64},{64,128},{128,192},{192,0},{1,65},{65,129},{129,193},{193,1... | collective-permute-start | bytes 786440 | tf_op jit(solution)/shard_map/ppermute | solution.py:19
  327.8 3.3 collective-permute-done.2
  (23 shorter events, 1.4 us)
Async XLA Ops:
  6.5 263.9 %copy-start = (bf16[1,1024,1024]{2,1,0:T(8,128)(2,1)S(1)}, bf16[1,1024,1024]{2,1,0:T(8,128)(2,1)}, u32[]{:S(2)}) copy-start(bf16[1,1024,1024]{2,1,0:T(8,128)(2,1)} %param.11) | copy-start | bytes 6291460
  6.5 61.3 %all-gather.3.cloned.1.call-start = ((), (), s32[]{:S(2)}) async-start(), calls=%async_computation.2 | async-start | bytes 2359296 | tf_op jit(solution)/shard_map/all_gather | solution.py:43
  27.1 130.4 %reduce-scatter.3.cloned.1.call-start = ((), (), s32[]{:S(2)}) async-start(), calls=%async_computation.3 | async-start | bytes 7077888 | tf_op jit(solution)/shard_map/reduce_scatter | solution.py:53
  79.2 191.2 %all-gather.5.cloned.1.call-start = ((), (), s32[]{:S(2)}) async-start(), calls=%async_computation.4 | async-start | bytes 2359296 | tf_op jit(solution)/shard_map/all_gather | solution.py:70
  159.7 22.9 %collective-permute-start = (bf16[127,3072]{1,0:T(8,128)(2,1)}, bf16[127,3072]{1,0:T(8,128)(2,1)}, u32[]{:S(2)}, u32[]{:S(2)}) collective-permute-start(bf16[127,3072]{1,0:T(8,128)(2,1)} %slice.24), channel_id=1, source_target_pairs={{0,8},{8,16},{16,24},{24,32},{32,40},{40,48},{48,56},{1,9},{9,17},... | collective-permute-start | bytes 2340872 | tf_op jit(solution)/shard_map/ppermute | solution.py:13
  177.9 4.6 %copy-start.1 = (bf16[128,3072]{1,0:T(8,128)(2,1)S(1)}, bf16[128,3072]{1,0:T(8,128)(2,1)}, u32[]{:S(2)}) copy-start(bf16[128,3072]{1,0:T(8,128)(2,1)} %reduce-scatter.3.cloned.1.call-done) | copy-start | bytes 2359300
  182.5 1.6 copy-start.3
  206.1 5.4 %copy-start.4 = (bf16[1,128,1024]{2,1,0:T(8,128)(2,1)S(1)}, bf16[1,128,1024]{2,1,0:T(8,128)(2,1)}, u32[]{:S(2)}) copy-start(bf16[1,128,1024]{2,1,0:T(8,128)(2,1)} %param.10) | copy-start | bytes 786436
  209.2 6.5 %collective-permute-start.1 = (bf16[127,1024]{0,1:T(8,128)(2,1)}, bf16[127,1024]{0,1:T(8,128)(2,1)}, u32[]{:S(2)}, u32[]{:S(2)}) collective-permute-start(bf16[127,1024]{0,1:T(8,128)(2,1)} %slice_bitcast_fusion), channel_id=1, source_target_pairs={{0,8},{8,16},{16,24},{24,32},{32,40},{40,48},{48,56},{1,9},{9,17},... | collective-permute-start | bytes 780296 | tf_op jit(solution)/shard_map/ppermute | solution.py:13
  227.1 91.7 %reduce-scatter.5.cloned.1.call-start = ((), (), s32[]{:S(2)}) async-start(), calls=%async_computation.5 | async-start | bytes 2359296 | tf_op jit(solution)/shard_map/reduce_scatter | solution.py:74
  275.7 43.2 %copy-start.2 = (bf16[1,128,1024]{2,1,0:T(8,128)(2,1)S(1)}, bf16[1,128,1024]{2,1,0:T(8,128)(2,1)}, u32[]{:S(2)}) copy-start(bf16[1,128,1024]{2,1,0:T(8,128)(2,1)} %param.6) | copy-start | bytes 786436
  319.8 11.3 %collective-permute-start.2 = (bf16[128,1024]{1,0:T(8,128)(2,1)S(1)}, bf16[128,1024]{1,0:T(8,128)(2,1)S(1)}, u32[]{:S(2)}, u32[]{:S(2)}) collective-permute-start(bf16[128,1024]{1,0:T(8,128)(2,1)S(1)} %fusion.10), channel_id=1, source_target_pairs={{0,64},{64,128},{128,192},{192,0},{1,65},{65,129},{129,193},{193,1... | collective-permute-start | bytes 786440 | tf_op jit(solution)/shard_map/ppermute | solution.py:19
Sparse Core Ops, SparseCore 0:
  27.2 40.6 all-gather.2
  79.3 78.1 reduce-scatter.2
  227.2 43.1 all-gather.4
  275.8 42.9 reduce-scatter.4
where the time goes:
time: 340 us; the launch traced here: 338 us
  waiting for transfers between devices  200 us (59%)
  local copies, waits for them, and re-layouts  42.4 us (12%)
  matrix products  41.3 us (12%)
  blocking collectives  16.8 us (5%)
  between operations  13.2 us (4%)
  starting transfers between devices  12.5 us (4%)
  other arithmetic  11.7 us (3%)
    reduce_scatter x1, waiting for transfers between devices, on_device(): lax.psum_scatter(jnp.dot(gathered, weight_in, preferred_element_type=jnp....  78.2 us
    all_gather x1, waiting for transfers between devices, on_device(): lax.all_gather(gated_out, 'ctx', axis=0, tiled=True)  43.2 us
    reduce_scatter x1, waiting for transfers between devices, on_device(): lax.psum_scatter(partial_value.astype(jnp.bfloat16), 'tp', scatter_dimens...  43.1 us
    all_gather x1, waiting for transfers between devices, on_device(): gathered = lax.all_gather(normed, 'tp', axis=0, tiled=True)  32.1 us
    conv_general_dilated x2, matrix products, causal_mix(): lax.conv_general_dilated(padded[None], kernel, (1,), 'VALID', dimension_n...  24.8 us
    psum x1, blocking collectives, on_device(): squares = lax.psum(jnp.sum(incoming * incoming, axis=1), 'ctx')  16.8 us
    rev x2, local copies, waits for them, and re-layouts, causal_mix(): kernel = tap_weights[::-1][:, None, :]  16 us
    unnamed x14, local copies, waits for them, and re-layouts  12.3 us
  transfers between devices with their start and end apart: 7, of which 6 were waited for; matrix products, arithmetic and copies ran while one was open for 10% of the time, Pallas kernels for 0%

commit v1 on v0

--- a/solution.py
+++ b/solution.py
@@ -67,7 +67,9 @@
     )
     gated_out = (filtered[:, 0] * mixed_sig).astype(jnp.bfloat16)
     partial_value = jnp.dot(
-        lax.all_gather(gated_out, "ctx", axis=0, tiled=True),
+        jnp.concatenate(
+            lax.all_to_all(jnp.stack([gated_out] * lax.axis_size("ctx")), "ctx", 0, 0), axis=0
+        ),
         weight_out,
         preferred_element_type=jnp.float32,
     )

time: 340 us -> 322 us (0.947)
  waiting for transfers between devices: 200 us -> 154 us
  blocking collectives: 16.8 us -> 47.4 us
    all_gather x1 -> x0, waiting for transfers between devices: 43.2 us -> none  [on_device(): lax.all_gather(gated_out, 'ctx', axis=0, tiled=True)]
    all_to_all x0 -> x1, blocking collectives: none -> 30.7 us  [on_device(): lax.all_to_all(jnp.stack([gated_out] * lax.axis_size('ctx')), 'ctx', 0, 0)]
    unnamed x14 -> x17, local copies, waits for them, and re-layouts: 12.3 us -> 12.2 us
  transfers between devices with their start and end apart: 7 -> 6, of which waited for: 6 -> 5; matrix products, arithmetic and copies ran while one was open for 10% -> 10% of each run, Pallas kernels for 0% -> 0%
where the time goes in v1:
time: 322 us; the launch traced here: 320 us
  waiting for transfers between devices  154 us (48%)
  blocking collectives  47.4 us (15%)
  local copies, waits for them, and re-layouts  42.6 us (13%)
  matrix products  40 us (12%)
  between operations  13.2 us (4%)
  starting transfers between devices  12.5 us (4%)
  other arithmetic  10.2 us (3%)
    reduce_scatter x1, waiting for transfers between devices, on_device(): lax.psum_scatter(jnp.dot(gathered, weight_in, preferred_element_type=jnp....  78.2 us
    reduce_scatter x1, waiting for transfers between devices, on_device(): lax.psum_scatter(partial_value.astype(jnp.bfloat16), 'tp', scatter_dimens...  40.3 us
    all_gather x1, waiting for transfers between devices, on_device(): gathered = lax.all_gather(normed, 'tp', axis=0, tiled=True)  32.1 us
    all_to_all x1, blocking collectives, on_device(): lax.all_to_all(jnp.stack([gated_out] * lax.axis_size('ctx')), 'ctx', 0, 0)  30.7 us
    conv_general_dilated x2, matrix products, causal_mix(): lax.conv_general_dilated(padded[None], kernel, (1,), 'VALID', dimension_n...  25 us
    psum x1, blocking collectives, on_device(): squares = lax.psum(jnp.sum(incoming * incoming, axis=1), 'ctx')  16.8 us
    rev x2, local copies, waits for them, and re-layouts, causal_mix(): kernel = tap_weights[::-1][:, None, :]  16 us
    unnamed x17, local copies, waits for them, and re-layouts  12.2 us
  transfers between devices with their start and end apart: 6, of which 5 were waited for; matrix products, arithmetic and copies ran while one was open for 10% of the time, Pallas kernels for 0%

profile of v1, /device:TPU:1, one launch (start us, length us, event | category | flops | bytes accessed | tf_op | source)
XLA Modules:
  0.0 320.3 jit_solution(2840708281400749232)
XLA Ops:
  6.5 0.8 mul.41
  7.4 1.1 fusion.8
  8.5 16.8 %psum.7 = f32[128]{0:T(128)S(1)} all-reduce(f32[128]{0:T(128)S(1)} %fusion.8), channel_id=1, replica_groups=mesh['pipe'=4,'ctx'=8,'tp'=8] {'ctx'}, use_global_device_ids=true, to_apply=%region_1.0 | all-reduce | flops 128 | bytes 1024 | tf_op jit(solution)/shard_map/psum | solution.py:39
  25.2 1.8 fusion.10
  27.1 8.7 %copy.11 = bf16[1,1024,3,1024]{1,3,2,0:T(8,128)(2,1)} copy(bf16[1,1024,3,1024]{3,1,2,0:T(8,128)(2,1)} %param.8) | data formatting | bytes 12582912 | tf_op args[2]
  35.8 32.1 %all-gather.2.cloned.1.call-done = bf16[1024,1024]{1,0:T(8,128)(2,1)} async-done(((bf16[128,1024]{1,0:T(8,128)(2,1)}), bf16[1024,1024]{1,0:T(8,128)(2,1)}) %all-gather.2.cloned.1.call-update) | async-done | bytes 2097168 | tf_op jit(solution)/shard_map/all_gather | solution.py:43
  67.9 11.2 %convolution_convert_fusion = bf16[1024,3072]{1,0:T(8,128)(2,1)} fusion(bf16[1024,1024]{1,0:T(8,128)(2,1)} %all-gather.2.cloned.1.call-done, bf16[1024,3072]{0,1:T(8,128)(2,1)} %bitcast.43), kind=kOutput, calls=%fused_computation | convolution fusion | flops 6445596672 | bytes 14680064 | tf_op jit(solution)/shard_map/dot_general | solution.py:54
  79.2 78.2 %reduce-scatter.3.cloned.1.call-done = bf16[128,3072]{1,0:T(8,128)(2,1)} async-done(((bf16[1024,3072]{1,0:T(8,128)(2,1)}), bf16[128,3072]{1,0:T(8,128)(2,1)}) %reduce-scatter.3.cloned.1.call-update) | async-done | bytes 786448 | tf_op jit(solution)/shard_map/reduce_scatter | solution.py:53
  157.4 2.2 slice.24
  159.6 2.2 collective-permute-start
  161.8 1.5 copy.12
  163.3 1.3 bitcast_convert_fusion
  164.5 13.3 %rev.6 = f32[128,3072]{0,1:T(8,128)} reverse(f32[128,3072]{0,1:T(8,128)} %bitcast.45), dimensions={0} | reverse | bytes 3145728 | tf_op jit(solution)/shard_map/rev | solution.py:24
  177.9 4.5 %copy.14 = f32[128,1,3072]{2,1,0:T(1,128)} copy(f32[128,1,3072]{0,2,1:T(8,128)} %bitcast.46) | data formatting | bytes 3145728 | tf_op jit(solution)/shard_map/broadcast_in_dim | solution.py:24
  182.5 1.5 maximum_bitcast_fusion
  184.1 17.5 %fusion = f32[1,128,3072]{2,0,1:T(1,128)} fusion(f32[128,1,3072]{2,1,0:T(1,128)S(1)} %copy-done.3, bf16[1,255,3072]{2,1,0:T(8,128)(2,1)S(1)} %maximum_bitcast_fusion), kind=kOutput, calls=%fused_computation.1 | convolution fusion | flops 603979776 | bytes 4712448 | tf_op jit(solution)/shard_map/conv_general_dilated | solution.py:25
  201.6 4.5 %copy.15 = f32[1,128,3072]{1,2,0:T(8,128)} copy(f32[1,128,3072]{2,0,1:T(1,128)} %fusion) | data formatting | bytes 3145728 | tf_op jit(solution)/shard_map/conv_general_dilated | solution.py:25
  206.0 1.5 fusion.14
  207.5 0.8 slice_bitcast_fusion
  208.4 2.3 collective-permute-start.1
  210.7 2.7 rev.7
  213.4 1.1 copy.23
  214.9 1.2 maximum_bitcast_fusion.1
  216.1 2.1 copy.18
  218.2 7.5 %fusion.7 = bf16[1,128,1024]{2,0,1:T(2,128)(2,1)S(1)} fusion(bf16[1,255,1024]{2,0,1:T(2,128)(2,1)} %copy.18, f32[128,1,1024]{2,1,0:T(1,128)} %copy.23, f32[128,1,1024]{2,0,1:T(8,128)S(1)} %bitcast.50), kind=kOutput, calls=%fused_computation.8 | convolution fusion | flops 201588736 | bytes 1832960 | tf_op jit(solution)/shard_map/conv_general_dilated | solution.py:25
  226.1 30.7 %all_to_all.5 = bf16[8,128,1024]{2,1,0:T(8,128)(2,1)S(1)} all-to-all(bf16[8,128,1024]{2,1,0:T(8,128)(2,1)S(1)} %stack.5), channel_id=1, replica_groups=mesh['pipe'=4,'ctx'=8,'tp'=8] {'ctx'}, dimensions={0} | all-to-all | bytes 4194304 | tf_op jit(solution)/shard_map/all_to_all | solution.py:71
  256.7 3.7 %fusion.4 = bf16[1024,1024]{1,0:T(8,128)(2,1)} fusion(bf16[1024,1024]{1,0:T(8,128)(2,1)S(1)} %bitcast.48, bf16[1,1024,1024]{2,1,0:T(8,128)(2,1)S(1)} %copy-done), kind=kOutput, calls=%fused_computation.5 | convolution fusion | flops 2148532224 | bytes 6291456 | tf_op jit(solution)/shard_map/dot_general | solution.py:69
  260.4 40.3 %reduce-scatter.5.cloned.1.call-done = bf16[128,1024]{1,0:T(8,128)(2,1)} async-done(((bf16[1024,1024]{1,0:T(8,128)(2,1)}), bf16[128,1024]{1,0:T(8,128)(2,1)}) %reduce-scatter.5.cloned.1.call-update) | async-done | bytes 262160 | tf_op jit(solution)/shard_map/reduce_scatter | solution.py:76
  300.7 1.0 fusion.11
  301.7 8.0 %collective-permute-start.2 = (bf16[128,1024]{1,0:T(8,128)(2,1)S(1)}, bf16[128,1024]{1,0:T(8,128)(2,1)S(1)}, u32[]{:S(2)}, u32[]{:S(2)}) collective-permute-start(bf16[128,1024]{1,0:T(8,128)(2,1)S(1)} %fusion.11), channel_id=1, source_target_pairs={{0,64},{64,128},{128,192},{192,0},{1,65},{65,129},{129,193},{193,1... | collective-permute-start | bytes 786440 | tf_op jit(solution)/shard_map/ppermute | solution.py:19
  309.7 3.3 %collective-permute-done.2 = bf16[128,1024]{1,0:T(8,128)(2,1)S(1)} collective-permute-done((bf16[128,1024]{1,0:T(8,128)(2,1)S(1)}, bf16[128,1024]{1,0:T(8,128)(2,1)S(1)}, u32[]{:S(2)}, u32[]{:S(2)}) %collective-permute-start.2) | collective-permute-done | bytes 262176 | tf_op jit(solution)/shard_map/ppermute | solution.py:19
  313.1 0.7 copy.31
  (24 shorter events, 1.1 us)
Async XLA Ops:
  6.5 250.2 %copy-start = (bf16[1,1024,1024]{2,1,0:T(8,128)(2,1)S(1)}, bf16[1,1024,1024]{2,1,0:T(8,128)(2,1)}, u32[]{:S(2)}) copy-start(bf16[1,1024,1024]{2,1,0:T(8,128)(2,1)} %param.11) | copy-start | bytes 6291460
  6.5 61.3 %all-gather.2.cloned.1.call-start = ((), (), s32[]{:S(2)}) async-start(), calls=%async_computation.3 | async-start | bytes 2359296 | tf_op jit(solution)/shard_map/all_gather | solution.py:43
  27.1 130.3 %reduce-scatter.3.cloned.1.call-start = ((), (), s32[]{:S(2)}) async-start(), calls=%async_computation.4 | async-start | bytes 7077888 | tf_op jit(solution)/shard_map/reduce_scatter | solution.py:53
  79.1 221.6 %reduce-scatter.5.cloned.1.call-start = ((), (), s32[]{:S(2)}) async-start(), calls=%async_computation.5 | async-start | bytes 2359296 | tf_op jit(solution)/shard_map/reduce_scatter | solution.py:76
  159.6 22.8 %collective-permute-start = (bf16[127,3072]{1,0:T(8,128)(2,1)}, bf16[127,3072]{1,0:T(8,128)(2,1)}, u32[]{:S(2)}, u32[]{:S(2)}) collective-permute-start(bf16[127,3072]{1,0:T(8,128)(2,1)} %slice.24), channel_id=1, source_target_pairs={{0,8},{8,16},{16,24},{24,32},{32,40},{40,48},{48,56},{1,9},{9,17},... | collective-permute-start | bytes 2340872 | tf_op jit(solution)/shard_map/ppermute | solution.py:13
  177.9 4.6 %copy-start.1 = (bf16[128,3072]{1,0:T(8,128)(2,1)S(1)}, bf16[128,3072]{1,0:T(8,128)(2,1)}, u32[]{:S(2)}) copy-start(bf16[128,3072]{1,0:T(8,128)(2,1)} %reduce-scatter.3.cloned.1.call-done) | copy-start | bytes 2359300
  182.4 1.6 copy-start.3
  206.0 4.6 %copy-start.5 = (bf16[1,128,1024]{2,1,0:T(8,128)(2,1)S(1)}, bf16[1,128,1024]{2,1,0:T(8,128)(2,1)}, u32[]{:S(2)}) copy-start(bf16[1,128,1024]{2,1,0:T(8,128)(2,1)} %param.10) | copy-start | bytes 786436
  208.4 6.5 %collective-permute-start.1 = (bf16[127,1024]{0,1:T(8,128)(2,1)}, bf16[127,1024]{0,1:T(8,128)(2,1)}, u32[]{:S(2)}, u32[]{:S(2)}) collective-permute-start(bf16[127,1024]{0,1:T(8,128)(2,1)} %slice_bitcast_fusion), channel_id=1, source_target_pairs={{0,8},{8,16},{16,24},{24,32},{32,40},{40,48},{48,56},{1,9},{9,17},... | collective-permute-start | bytes 780296 | tf_op jit(solution)/shard_map/ppermute | solution.py:13
  214.4 3.7 %copy-start.4 = (f32[128,1024]{1,0:T(8,128)S(1)}, f32[128,1024]{1,0:T(8,128)}, u32[]{:S(2)}) copy-start(f32[128,1024]{1,0:T(8,128)} %rev.7) | copy-start | bytes 1572868
  260.4 40.3 %copy-start.2 = (bf16[1,128,1024]{2,1,0:T(8,128)(2,1)S(1)}, bf16[1,128,1024]{2,1,0:T(8,128)(2,1)}, u32[]{:S(2)}) copy-start(bf16[1,128,1024]{2,1,0:T(8,128)(2,1)} %param.6) | copy-start | bytes 786436
  301.7 11.3 %collective-permute-start.2 = (bf16[128,1024]{1,0:T(8,128)(2,1)S(1)}, bf16[128,1024]{1,0:T(8,128)(2,1)S(1)}, u32[]{:S(2)}, u32[]{:S(2)}) collective-permute-start(bf16[128,1024]{1,0:T(8,128)(2,1)S(1)} %fusion.11), channel_id=1, source_target_pairs={{0,64},{64,128},{128,192},{192,0},{1,65},{65,129},{129,193},{193,1... | collective-permute-start | bytes 786440 | tf_op jit(solution)/shard_map/ppermute | solution.py:19
Sparse Core Ops, SparseCore 0:
  27.2 40.6 all-gather.1
  79.2 78.1 reduce-scatter.2
  260.6 40.1 reduce-scatter.4
